TPU v7x, 128 devices: a whole 4x4x4 slice. The times are simulated.
128 devices in a mesh: dp: 16 (over z_hi, x, core), tensor: 8 (over z_lo, y).
Axes of the slice: x: 4, y: 4, z: 4 (z_hi: 2, z_lo: 2; z = z_hi * 2 + z_lo), core: 2. Of those that a mesh axis runs over, the one named last changes fastest.
Arguments:
- tokens: bfloat16 [16384, 8192], P('dp', 'tensor'), may hold values from -6 to 6
- ref_gain: float32 [8192], P('tensor'), may hold values from 0.1 to 1.9
- ref_weight: bfloat16 [8192, 512], P('tensor'), may hold values from -0.0625 to 0.0625
- pol_gain: float32 [8192], replicated, may hold values from 0.1 to 1.9
- pol_weight: bfloat16 [8192, 512], P('dp'), may hold values from -0.0625 to 0.0625
- lengths: int32 [16, 8, 16], P('dp', 'tensor'), may hold values from 1 to 16, 128 in all within a row
- bins: int32 [16, 8, 16], P('dp', 'tensor'), may hold values from 0 to 15, each once within a row
- advantage: float32 [16, 8, 16], P('dp', 'tensor'), may hold values from -4 to 4
- logprob_gap: float32 [16384], P(('dp', 'tensor')), may hold values from -1 to 1
- cotangent: bfloat16 [16, 8, 256, 512], P('dp', 'tensor'), may hold values from -6 to 6
Outputs:
- policy_values: bfloat16 [16, 8, 256, 512], P('dp', 'tensor')
- grad_weight: float32 [8192, 512], P(('dp', 'tensor'))
Inputs may be any that keep to these rules, and one draw needn't show every extreme that they name: `lengths`: lengths of the 16 sequences of one run, in the order in which they lie in it; they sum to 128, and the longest of every run is exactly 16. The sequences of one run go to distinct bins: each bin takes exactly one sequence of every run.
All inputs are finite; a program needn't handle non-finite values.
Results may differ from a plain program's by a relative error of at most 0.015.
Values may be sent and summed in bfloat16 or wider, within the bound.
A program may use at most 64 MiB of HBM per device.

v0:
```python
import math
import jax
import jax.numpy as jnp
from jax import lax
from jax.sharding import PartitionSpec as P

EPS = 1e-06
BETA = 1.0


def rounded(values):
    return lax.optimization_barrier(values.astype(jnp.bfloat16)).astype(jnp.float32)


def on_device(
    tokens,
    ref_gain,
    ref_weight,
    pol_gain,
    pol_weight,
    lengths,
    bins,
    advantage,
    logprob_gap,
    cotangent,
):
    tensor_count = lax.axis_size("tensor")
    dp_count = lax.axis_size("dp")
    group_rows = tokens.shape[0]
    own_rows = group_rows // tensor_count
    slot_count = cotangent.shape[2]
    span_rows = slot_count // dp_count
    model_width = pol_gain.shape[0]
    value_width = ref_weight.shape[1]
    scaled = (tokens.astype(jnp.float32) * ref_gain[None, :]).astype(jnp.bfloat16)
    partial_value = rounded(jnp.dot(scaled, ref_weight, preferred_element_type=jnp.float32))
    summed = lax.psum(partial_value.astype(jnp.bfloat16), "tensor").astype(jnp.float32)
    owned_sum = lax.dynamic_slice_in_dim(summed, lax.axis_index("tensor") * own_rows, own_rows, 0)
    full_rows = lax.all_to_all(tokens, "tensor", split_axis=0, concat_axis=1, tiled=True)
    row_power = jnp.mean(jnp.square(full_rows.astype(jnp.float32)), axis=1)
    ref_values = (owned_sum * lax.rsqrt(row_power + EPS)[:, None]).astype(jnp.bfloat16)
    seq_lens = lengths.reshape(-1)
    seq_bins = bins.reshape(-1)
    seq_adv = advantage.reshape(-1)
    seq_starts = jnp.cumsum(seq_lens) - seq_lens
    chosen = seq_bins[None, :] == jnp.arange(dp_count, dtype=jnp.int32)[:, None]
    bin_len = jnp.sum(jnp.where(chosen, seq_lens[None, :], 0), axis=1)
    bin_start = jnp.sum(jnp.where(chosen, seq_starts[None, :], 0), axis=1)
    bin_adv = jnp.sum(jnp.where(chosen, seq_adv[None, :], jnp.float32(0.0)), axis=1)
    offsets = jnp.arange(span_rows, dtype=jnp.int32)
    usable = offsets[None, :] < bin_len[:, None]
    row_picks = jnp.clip(bin_start[:, None] + offsets[None, :], 0, own_rows - 1)
    send_rows = jnp.where(usable[:, :, None], full_rows[row_picks], jnp.zeros((), jnp.bfloat16))
    send_ref = jnp.where(usable[:, :, None], ref_values[row_picks], jnp.zeros((), jnp.bfloat16))
    len_float = bin_len.astype(jnp.float32)[:, None]
    importance = jnp.minimum(jnp.exp(logprob_gap[row_picks]), jnp.float32(2.0))
    coef_adv = jnp.where(
        usable, bin_adv[:, None] * importance / len_float, jnp.float32(0.0)
    ).astype(jnp.bfloat16)
    coef_pull = jnp.where(usable, BETA / len_float, jnp.float32(0.0)).astype(jnp.bfloat16)
    got_rows, got_ref, got_adv, got_pull = (
        lax.all_to_all(send_rows, "dp", split_axis=0, concat_axis=0, tiled=True),
        lax.all_to_all(send_ref, "dp", split_axis=0, concat_axis=0, tiled=True),
        lax.all_to_all(coef_adv, "dp", split_axis=0, concat_axis=0, tiled=True),
        lax.all_to_all(coef_pull, "dp", split_axis=0, concat_axis=0, tiled=True),
    )
    packed_rows = got_rows.reshape(slot_count, model_width)
    power = jnp.mean(jnp.square(packed_rows.astype(jnp.float32)), axis=1)
    normed = (
        packed_rows.astype(jnp.float32) * lax.rsqrt(power + EPS)[:, None] * pol_gain[None, :]
    ).astype(jnp.bfloat16)
    packed_ref = got_ref.reshape(slot_count, value_width).astype(jnp.float32)
    adv_column = got_adv.reshape(slot_count, 1).astype(jnp.float32)
    pull_column = got_pull.reshape(slot_count, 1).astype(jnp.float32)
    upstream = cotangent.reshape(slot_count, value_width).astype(jnp.float32)
    factor = 1.0 / math.sqrt(dp_count * tensor_count * seq_lens.shape[0])
    feature_block = normed
    values = jnp.dot(
        feature_block,
        lax.all_gather(pol_weight, "dp", axis=0, tiled=True),
        preferred_element_type=jnp.float32,
    )
    slope = (adv_column * upstream + pull_column * (values - packed_ref)).astype(jnp.bfloat16)
    feature_block = normed
    grad_weight = lax.psum_scatter(
        lax.dot_general(
            feature_block, slope, (((0,), (0,)), ((), ())), preferred_element_type=jnp.float32
        )
        * factor,
        ("dp", "tensor"),
        scatter_dimension=0,
        tiled=True,
    )
    policy_values = values.astype(jnp.bfloat16).reshape(1, 1, slot_count, value_width)
    return (policy_values, grad_weight)


def solution(mesh):
    in_specs = (
        P("dp", "tensor"),
        P("tensor"),
        P("tensor", None),
        P(),
        P("dp", None),
        P("dp", "tensor", None),
        P("dp", "tensor", None),
        P("dp", "tensor", None),
        P(("dp", "tensor")),
        P("dp", "tensor", None, None),
    )
    out_specs = (P("dp", "tensor", None, None), P(("dp", "tensor"), None))
    return jax.shard_map(
        on_device, mesh=mesh, in_specs=in_specs, out_specs=out_specs, check_vma=False
    )
```

profile of v0, /device:TPU:0, one launch (start us, length us, event | category | flops | bytes accessed | tf_op | source)
XLA Modules:
  0.0 858.9 jit_solution(14189858339868962872)
XLA Ops:
  8.0 0.0 copy-start
  8.0 0.0 all-reduce.2.cloned.1.call-start
  8.1 1.2 copy-done
  9.2 3.8 fusion.4
  13.1 0.0 copy-start.6
  13.1 0.0 copy-start.7
  13.1 0.0 copy-start.1
  13.1 0.0 all-reduce.2.cloned.1.call-update
  13.1 0.0 all-gather.2.cloned.1.call-start
  13.1 0.5 all-gather.2.cloned.1.call-update
  13.7 5.9 all-to-all-start
  19.6 0.0 copy-done.6
  19.6 0.1 copy.19
  19.7 0.1 reduce.2
  19.8 0.0 copy-done.7
  19.9 0.1 select_reduce_fusion.2
  20.0 0.1 compare_select_fusion
  20.0 0.1 reshape.312
  20.1 0.0 copy-done.1
  20.2 0.0 copy-start.8
  20.2 1.9 gather_fusion.1
  22.1 0.1 min.28
  22.1 0.0 copy-done.8
  22.2 0.1 select_reduce_fusion
  22.3 0.7 fusion.12
  23.0 0.7 fusion.13
  23.7 27.8 %all-to-all-done = bf16[8,128,1024]{2,1,0:T(8,128)(2,1)S(1)} async-done(((bf16[8,128,1024]{2,1,0:T(8,128)(2,1)}), bf16[8,128,1024]{2,1,0:T(8,128)(2,1)S(1)}, u32[]{:S(2)}, u32[]{:S(2)}) %all-to-all-start) | async-done | bytes 2097184 | tf_op jit(solution)/shard_map/all_to_all | solution.py:39
  51.5 0.0 copy-start.2
  51.5 7.6 all-to-all-start.2
  59.1 0.1 iota_compare_fusion.1
  59.2 0.0 copy-done.2
  59.2 1.8 copy.20
  61.0 5.2 gather_fusion
  66.2 0.4 all-to-all-done.2
  66.6 6.8 all-to-all-start.3
  73.4 4.5 broadcast_select_fusion
  77.9 0.0 copy-start.3
  77.9 3.0 all-to-all-done.3
  80.9 4.5 all-to-all-start.1
  85.5 0.1 reshape.306
  85.6 0.1 reshape.308
  85.7 0.0 copy-done.3
  85.7 0.5 multiply_reduce_fusion.1
  86.2 0.0 copy-start.5
  86.2 29.8 %all-reduce.2.cloned.1.call-done = bf16[1024,512]{1,0:T(8,128)(2,1)} async-done(((bf16[1024,512]{1,0:T(8,128)(2,1)}), bf16[1024,512]{1,0:T(8,128)(2,1)}) %all-reduce.2.cloned.1.call-update) | async-done | bytes 1048592 | tf_op jit(solution)/shard_map/psum | solution.py:37
  116.1 1.0 multiply_convert_fusion.4
  117.1 1.2 gather_fusion.2
  118.2 0.8 broadcast_select_fusion.1
  119.0 32.7 %all-to-all-done.1 = bf16[16,16,8192]{2,1,0:T(8,128)(2,1)} async-done(((bf16[16,16,8192]{2,1,0:T(8,128)(2,1)}), bf16[16,16,8192]{2,1,0:T(8,128)(2,1)}, u32[]{:S(2)}, u32[]{:S(2)}) %all-to-all-start.1) | async-done | bytes 4194336 | tf_op jit(solution)/shard_map/all_to_all | solution.py:62
  151.7 4.4 all-to-all-start.4
  156.1 0.2 reduce-scatter.2.cloned.1.call-start
  156.3 3.2 multiply_reduce_fusion
  159.6 0.1 rsqrt.18
  159.7 0.0 copy-done.5
  159.7 5.3 fusion.1
  165.0 0.0 copy-start.4
  165.0 0.0 all-gather.2.cloned.1.call-done
  165.0 7.0 fusion.14
  172.1 0.0 all-to-all-done.4
  172.1 0.0 copy-done.4
  172.1 10.4 %convolution_multiply_fusion = f32[8192,512]{1,0:T(8,128)} fusion(bf16[256,8192]{1,0:T(8,128)(2,1)} %fusion.1, f32[256,512]{1,0:T(8,128)S(1)} %fusion.14, bf16[256,512]{1,0:T(8,128)(2,1)S(1)} %bitcast.38, bf16[1,1,256,512]{3,2,1,0:T(8,128)(2,1)S(1)} %copy-done.4, f32[256]{0:T(256)S(1)} %reshape.308, f32[256]{0:T(256)S(1)} %reshape.306), kind=kOutput, calls=%fused_computation.3 | convolution fusion | flops 2152595456 | bytes 22022144 | tf_op jit(solution)/shard_map/dot_general | solution.py:86
  182.5 0.0 reduce-scatter.2.cloned.1.call-update
  182.5 0.7 convert_bitcast_fusion
  183.2 668.2 %reduce-scatter.2.cloned.1.call-done = f32[64,512]{1,0:T(8,128)} async-done(((f32[8192,512]{1,0:T(8,128)}), f32[64,512]{1,0:T(8,128)}) %reduce-scatter.2.cloned.1.call-update) | async-done | bytes 131088 | tf_op jit(solution)/shard_map/reduce_scatter | solution.py:85
  (10 shorter events, 0.1 us)
Async XLA Ops:
  8.0 1.2 copy-start
  8.0 108.1 %all-reduce.2.cloned.1.call-start = ((), (), s32[]{:S(2)}) async-start(), calls=%async_computation.7 | async-start | bytes 2097152 | tf_op jit(solution)/shard_map/psum | solution.py:37
  13.1 6.5 copy-start.6
  13.1 6.8 copy-start.7
  13.1 7.1 copy-start.1
  13.1 151.9 %all-gather.2.cloned.1.call-start = ((), (), s32[]{:S(2)}) async-start(), calls=%async_computation.6 | async-start | bytes 8912896 | tf_op jit(solution)/shard_map/all_gather | solution.py:80
  13.7 37.9 %all-to-all-start = ((bf16[8,128,1024]{2,1,0:T(8,128)(2,1)}), bf16[8,128,1024]{2,1,0:T(8,128)(2,1)S(1)}, u32[]{:S(2)}, u32[]{:S(2)}) async-start(bf16[8,128,1024]{2,1,0:T(8,128)(2,1)} %bitcast.37), calls=%async_computation | async-start | bytes 4194304 | tf_op jit(solution)/shard_map/all_to_all | solution.py:39
  20.2 2.0 copy-start.8
  51.5 7.7 copy-start.2
  51.5 15.1 %all-to-all-start.2 = ((bf16[16,1,16]{2,1,0:T(2,128)(2,1)}), bf16[16,1,16]{2,1,0:T(2,128)(2,1)S(1)}, u32[]{:S(2)}, u32[]{:S(2)}) async-start(bf16[16,1,16]{2,1,0:T(2,128)(2,1)} %fusion.13), calls=%async_computation.2 | async-start | bytes 16384 | tf_op jit(solution)/shard_map/all_to_all | solution.py:64
  66.6 14.3 %all-to-all-start.3 = ((bf16[16,1,16]{2,1,0:T(2,128)(2,1)}), bf16[16,1,16]{2,1,0:T(2,128)(2,1)S(1)}, u32[]{:S(2)}, u32[]{:S(2)}) async-start(bf16[16,1,16]{2,1,0:T(2,128)(2,1)} %fusion.12), calls=%async_computation.3 | async-start | bytes 16384 | tf_op jit(solution)/shard_map/all_to_all | solution.py:65
  77.9 7.8 copy-start.3
  80.9 70.8 %all-to-all-start.1 = ((bf16[16,16,8192]{2,1,0:T(8,128)(2,1)}), bf16[16,16,8192]{2,1,0:T(8,128)(2,1)}, u32[]{:S(2)}, u32[]{:S(2)}) async-start(bf16[16,16,8192]{2,1,0:T(8,128)(2,1)} %broadcast_select_fusion), calls=%async_computation.1 | async-start | bytes 8388608 | tf_op jit(solution)/shard_map/all_to_all | solution.py:62
  86.2 73.5 %copy-start.5 = (f32[8192]{0:T(1024)S(1)}, f32[8192]{0:T(1024)}, u32[]{:S(2)}) copy-start(f32[8192]{0:T(1024)} %param.13) | copy-start | bytes 98308
  151.7 20.3 %all-to-all-start.4 = ((bf16[16,16,512]{2,1,0:T(8,128)(2,1)}), bf16[16,16,512]{2,1,0:T(8,128)(2,1)S(1)}, u32[]{:S(2)}, u32[]{:S(2)}) async-start(bf16[16,16,512]{2,1,0:T(8,128)(2,1)} %broadcast_select_fusion.1), calls=%async_computation.4 | async-start | bytes 524288 | tf_op jit(solution)/shard_map/all_to_all | solution.py:63
  156.1 695.3 %reduce-scatter.2.cloned.1.call-start = ((), (), s32[]{:S(2)}) async-start(), calls=%async_computation.8 | async-start | bytes 16908288 | tf_op jit(solution)/shard_map/reduce_scatter | solution.py:85
  165.0 7.0 copy-start.4
Sparse Core Ops, SparseCore 0:
  13.2 102.8 all-reduce.1
  182.6 668.7 reduce-scatter.1
Sparse Core Ops, SparseCore 1:
  16.0 145.2 all-gather.1
where the time goes:
time: 860 us; the launch traced here: 859 us
  waiting for transfers between devices  763 us (89%)
  starting transfers between devices  29.6 us (3%)
  matrix products  21.2 us (2%)
  other arithmetic  18.1 us (2%)
  between operations  15.7 us (2%)
  local copies, waits for them, and re-layouts  11.7 us (1%)
    reduce_scatter x1, waiting for transfers between devices, on_device(): lax.psum_scatter(lax.dot_general(feature_block, slope, (((0,), (0,)), (()...  668 us
    all_to_all x1, waiting for transfers between devices, on_device(): lax.all_to_all(send_rows, 'dp', split_axis=0, concat_axis=0, tiled=True)  32.7 us
    psum x1, waiting for transfers between devices, on_device(): lax.psum(partial_value.astype(jnp.bfloat16), 'tensor').astype(jnp.float32)  29.8 us
    all_to_all x1, waiting for transfers between devices, on_device(): lax.all_to_all(tokens, 'tensor', split_axis=0, concat_axis=1, tiled=True)  27.8 us
  transfers between devices with their start and end apart: 8, of which 6 were waited for; matrix products, arithmetic and copies ran while one was open for 4% of the time, Pallas kernels for 0%

commit v1 on v0

--- a/solution.py
+++ b/solution.py
@@ -6,6 +6,13 @@
 
 EPS = 1e-06
 BETA = 1.0
+
+
+def swap_blocks(block, mesh_axis, split, join):
+    n_dev = lax.axis_size(mesh_axis)
+    blocks = jnp.stack(jnp.split(block, n_dev, axis=split), axis=0)
+    blocks = lax.all_to_all(blocks, mesh_axis, split_axis=0, concat_axis=0)
+    return jnp.concatenate(blocks, axis=join)
 
 
 def rounded(values):
@@ -36,7 +43,7 @@
     partial_value = rounded(jnp.dot(scaled, ref_weight, preferred_element_type=jnp.float32))
     summed = lax.psum(partial_value.astype(jnp.bfloat16), "tensor").astype(jnp.float32)
     owned_sum = lax.dynamic_slice_in_dim(summed, lax.axis_index("tensor") * own_rows, own_rows, 0)
-    full_rows = lax.all_to_all(tokens, "tensor", split_axis=0, concat_axis=1, tiled=True)
+    full_rows = swap_blocks(tokens, "tensor", 0, 1)
     row_power = jnp.mean(jnp.square(full_rows.astype(jnp.float32)), axis=1)
     ref_values = (owned_sum * lax.rsqrt(row_power + EPS)[:, None]).astype(jnp.bfloat16)
     seq_lens = lengths.reshape(-1)

time: 860 us -> 868 us (level)
  transfers between devices with their start and end apart: 8 -> 8, of which waited for: 6 -> 6; matrix products, arithmetic and copies ran while one was open for 4% -> 5% of each run, Pallas kernels for 0% -> 0%
where the time goes in v1:
time: 868 us
  waiting for transfers between devices  761 us (88%)
  starting transfers between devices  34.2 us (4%)
  matrix products  21.2 us (2%)
  other arithmetic  18 us (2%)
  local copies, waits for them, and re-layouts  17.6 us (2%)
  between operations  15.7 us (2%)
    reduce_scatter x1, waiting for transfers between devices, on_device(): lax.psum_scatter(lax.dot_general(feature_block, slope, (((0,), (0,)), (()...  667 us
    all_to_all x1, waiting for transfers between devices, on_device(): lax.all_to_all(send_rows, 'dp', split_axis=0, concat_axis=0, tiled=True)  34.8 us
    all_to_all x1, waiting for transfers between devices, swap_blocks(): blocks = lax.all_to_all(blocks, mesh_axis, split_axis=0, concat_axis=0)  31.1 us
    psum x1, waiting for transfers between devices, on_device(): lax.psum(partial_value.astype(jnp.bfloat16), 'tensor').astype(jnp.float32)  23.8 us
  transfers between devices with their start and end apart: 8, of which 6 were waited for; matrix products, arithmetic and copies ran while one was open for 5% of the time, Pallas kernels for 0%

profile of v1, /device:TPU:0, one launch (start us, length us, event | category | flops | bytes accessed | tf_op | source)
XLA Modules:
  0.0 867.6 jit_solution(14260503860598000691)
XLA Ops:
  8.0 0.0 copy-start
  8.0 0.0 copy-start.4
  8.0 0.0 all-reduce.2.cloned.1.call-start
  8.1 1.2 copy-done
  9.2 3.8 fusion.4
  13.1 0.0 all-reduce.2.cloned.1.call-update
  13.1 0.0 all-gather.2.cloned.1.call-start
  13.1 0.5 all-gather.2.cloned.1.call-update
  13.7 0.0 copy-done.4
  13.7 0.7 bitcast_dynamic-update-slice_fusion.7
  14.4 0.7 bitcast_dynamic-update-slice_fusion.6
  15.1 0.7 bitcast_dynamic-update-slice_fusion.5
  15.9 0.7 bitcast_dynamic-update-slice_fusion.4
  16.6 0.7 bitcast_dynamic-update-slice_fusion.3
  17.3 0.7 bitcast_dynamic-update-slice_fusion.2
  18.1 0.7 bitcast_dynamic-update-slice_fusion.1
  18.8 0.7 bitcast_dynamic-update-slice_fusion
  19.5 6.0 all-to-all-start
  25.6 0.0 copy-done.7
  25.6 0.1 copy.17
  25.7 0.1 reduce.2
  25.8 0.0 copy-done.8
  25.8 0.1 select_reduce_fusion.2
  25.9 0.1 compare_select_fusion
  26.0 0.1 reshape.317
  26.1 0.0 copy-done.1
  26.1 0.0 copy-start.9
  26.1 1.9 gather_fusion.1
  28.0 0.1 min.28
  28.1 0.0 copy-done.9
  28.1 0.1 select_reduce_fusion
  28.3 0.7 fusion.12
  29.0 0.7 fusion.13
  29.7 31.1 %all-to-all-done = bf16[8,128,1024]{2,1,0:T(8,128)(2,1)S(1)} async-done(((bf16[8,128,1024]{2,1,0:T(8,128)(2,1)}), bf16[8,128,1024]{2,1,0:T(8,128)(2,1)S(1)}, u32[]{:S(2)}, u32[]{:S(2)}) %all-to-all-start) | async-done | bytes 2097184 | tf_op jit(solution)/shard_map/all_to_all | solution.py:14
  60.8 7.5 all-to-all-start.2
  68.2 0.1 iota_compare_fusion.1
  68.3 1.8 copy.18
  70.2 5.2 gather_fusion
  75.3 0.4 all-to-all-done.2
  75.7 6.8 all-to-all-start.3
  82.6 4.6 broadcast_select_fusion
  87.1 2.9 all-to-all-done.3
  90.0 4.6 all-to-all-start.1
  94.7 0.1 reshape.311
  94.8 0.1 reshape.313
  94.9 0.5 multiply_reduce_fusion.1
  95.4 23.8 %all-reduce.2.cloned.1.call-done = bf16[1024,512]{1,0:T(8,128)(2,1)} async-done(((bf16[1024,512]{1,0:T(8,128)(2,1)}), bf16[1024,512]{1,0:T(8,128)(2,1)}) %all-reduce.2.cloned.1.call-update) | async-done | bytes 1048592 | tf_op jit(solution)/shard_map/psum | solution.py:44
  119.1 1.0 multiply_convert_fusion.4
  120.1 1.2 gather_fusion.2
  121.3 0.8 broadcast_select_fusion.1
  122.1 34.8 %all-to-all-done.1 = bf16[16,16,8192]{2,1,0:T(8,128)(2,1)} async-done(((bf16[16,16,8192]{2,1,0:T(8,128)(2,1)}), bf16[16,16,8192]{2,1,0:T(8,128)(2,1)}, u32[]{:S(2)}, u32[]{:S(2)}) %all-to-all-start.1) | async-done | bytes 4194336 | tf_op jit(solution)/shard_map/all_to_all | solution.py:69
  156.9 9.0 %all-to-all-start.4 = ((bf16[16,16,512]{2,1,0:T(8,128)(2,1)}), bf16[16,16,512]{2,1,0:T(8,128)(2,1)S(1)}, u32[]{:S(2)}, u32[]{:S(2)}) async-start(bf16[16,16,512]{2,1,0:T(8,128)(2,1)} %broadcast_select_fusion.1), calls=%async_computation.4 | async-start | bytes 524288 | tf_op jit(solution)/shard_map/all_to_all | solution.py:70
  166.0 0.0 copy-start.6
  166.0 0.2 reduce-scatter.2.cloned.1.call-start
  166.2 3.1 multiply_reduce_fusion
  169.3 0.1 rsqrt.18
  169.4 5.3 fusion.1
  174.7 7.0 fusion.14
  181.7 0.0 all-to-all-done.4
  181.7 0.0 copy-done.5
  181.7 10.4 %convolution_multiply_fusion = f32[8192,512]{1,0:T(8,128)} fusion(bf16[256,8192]{1,0:T(8,128)(2,1)} %fusion.1, f32[256,512]{1,0:T(8,128)S(1)} %fusion.14, bf16[256,512]{1,0:T(8,128)(2,1)S(1)} %bitcast.52, bf16[1,1,256,512]{3,2,1,0:T(8,128)(2,1)S(1)} %copy-done.5, f32[256]{0:T(256)S(1)} %reshape.313, f32[256]{0:T(256)S(1)} %reshape.311), kind=kOutput, calls=%fused_computation.3 | convolution fusion | flops 2152595456 | bytes 22022144 | tf_op jit(solution)/shard_map/dot_general | solution.py:93
  192.1 0.0 reduce-scatter.2.cloned.1.call-update
  192.1 0.7 convert_bitcast_fusion
  192.9 667.3 %reduce-scatter.2.cloned.1.call-done = f32[64,512]{1,0:T(8,128)} async-done(((f32[8192,512]{1,0:T(8,128)}), f32[64,512]{1,0:T(8,128)}) %reduce-scatter.2.cloned.1.call-update) | async-done | bytes 131088 | tf_op jit(solution)/shard_map/reduce_scatter | solution.py:92
  (20 shorter events, 0.2 us)
Async XLA Ops:
  8.0 1.2 copy-start
  8.0 5.7 copy-start.4
  8.0 111.1 %all-reduce.2.cloned.1.call-start = ((), (), s32[]{:S(2)}) async-start(), calls=%async_computation.7 | async-start | bytes 2097152 | tf_op jit(solution)/shard_map/psum | solution.py:44
  13.1 161.6 %all-gather.2.cloned.1.call-start = ((), (), s32[]{:S(2)}) async-start(), calls=%async_computation.6 | async-start | bytes 8912896 | tf_op jit(solution)/shard_map/all_gather | solution.py:87
  19.5 6.0 copy-start.7
  19.5 6.3 copy-start.8
  19.5 6.6 copy-start.1
  19.5 41.2 %all-to-all-start = ((bf16[8,128,1024]{2,1,0:T(8,128)(2,1)}), bf16[8,128,1024]{2,1,0:T(8,128)(2,1)S(1)}, u32[]{:S(2)}, u32[]{:S(2)}) async-start(bf16[8,128,1024]{2,1,0:T(8,128)(2,1)} %bitcast_dynamic-update-slice_fusion), calls=%async_computation | async-start | bytes 4194304 | tf_op jit(solution)/shard_map/all_to_all | solution.py:14
  26.1 2.0 copy-start.9
  60.8 7.6 copy-start.2
  60.8 15.0 %all-to-all-start.2 = ((bf16[16,1,16]{2,1,0:T(2,128)(2,1)}), bf16[16,1,16]{2,1,0:T(2,128)(2,1)S(1)}, u32[]{:S(2)}, u32[]{:S(2)}) async-start(bf16[16,1,16]{2,1,0:T(2,128)(2,1)} %fusion.13), calls=%async_computation.2 | async-start | bytes 16384 | tf_op jit(solution)/shard_map/all_to_all | solution.py:71
  75.7 14.3 %all-to-all-start.3 = ((bf16[16,1,16]{2,1,0:T(2,128)(2,1)}), bf16[16,1,16]{2,1,0:T(2,128)(2,1)S(1)}, u32[]{:S(2)}, u32[]{:S(2)}) async-start(bf16[16,1,16]{2,1,0:T(2,128)(2,1)} %fusion.12), calls=%async_computation.3 | async-start | bytes 16384 | tf_op jit(solution)/shard_map/all_to_all | solution.py:72
  87.1 7.8 copy-start.3
  90.0 66.9 %all-to-all-start.1 = ((bf16[16,16,8192]{2,1,0:T(8,128)(2,1)}), bf16[16,16,8192]{2,1,0:T(8,128)(2,1)}, u32[]{:S(2)}, u32[]{:S(2)}) async-start(bf16[16,16,8192]{2,1,0:T(8,128)(2,1)} %broadcast_select_fusion), calls=%async_computation.1 | async-start | bytes 8388608 | tf_op jit(solution)/shard_map/all_to_all | solution.py:69
  156.9 24.8 %all-to-all-start.4 = ((bf16[16,16,512]{2,1,0:T(8,128)(2,1)}), bf16[16,16,512]{2,1,0:T(8,128)(2,1)S(1)}, u32[]{:S(2)}, u32[]{:S(2)}) async-start(bf16[16,16,512]{2,1,0:T(8,128)(2,1)} %broadcast_select_fusion.1), calls=%async_computation.4 | async-start | bytes 524288 | tf_op jit(solution)/shard_map/all_to_all | solution.py:70
  166.0 3.4 copy-start.6
  166.0 694.2 %reduce-scatter.2.cloned.1.call-start = ((), (), s32[]{:S(2)}) async-start(), calls=%async_computation.8 | async-start | bytes 16908288 | tf_op jit(solution)/shard_map/reduce_scatter | solution.py:92
  174.7 7.0 copy-start.5
Sparse Core Ops, SparseCore 0:
  13.2 105.8 all-reduce.1
  192.3 667.8 reduce-scatter.1
Sparse Core Ops, SparseCore 1:
  16.0 147.6 all-gather.1
